TPU v7x, 256 devices: a whole 4x4x8 slice. The times are simulated.
256 devices in a mesh: pts: 256 (over y, x, z, core).
Axes of the slice: x: 4, y: 4, z: 8, core: 2. Of those that a mesh axis runs over, the one named last changes fastest.
Arguments:
- rhs: float32 [64, 262144], P(None, 'pts'), may hold values from -6 to 6
- ridge: float32 [262144], P('pts'), may hold values from 0.1 to 2
- leaf_basis: float32 [1024, 256, 256], P('pts'), may hold values from -0.375 to 0.375
- leaf_transfer: float32 [1024, 256, 256], P('pts'), may hold values from -0.1875 to 0.1875
- near_blocks: float32 [1024, 3, 256, 256], P('pts'), may hold values from -0.375 to 0.375
- near_list: int32 [1024, 3], P('pts'), may hold values from 0 to 1023, as said below
- leaf_coupling: float32 [1024, 4, 256, 256], P('pts'), may hold values from -0.1875 to 0.1875
- leaf_far: int32 [1024, 4], P('pts'), may hold values from 0 to 1023, as said below
- node_coupling: float32 [256, 6, 256, 256], P('pts'), may hold values from -0.15625 to 0.15625
- node_far: int32 [256, 6], P('pts'), may hold values from 0 to 255, as said below
Outputs:
- product: float32 [64, 262144], P(None, 'pts')
Inputs may be any that keep to these rules, and one draw needn't show every extreme that they name: `near_list`: entry 0 of each row is the leaf itself; the others are leaves 1 to 4 places away from it. `leaf_far`: leaves 1 to 4 places away from the row's leaf. `node_far`: First-level nodes 2 to 4 places away from the row's node; entries may repeat in rows near the ends.
All inputs are finite; a program needn't handle non-finite values.
Results may differ from a plain program's by a relative error of at most 0.000054.
Values sent between devices are 32-bit elements; how exact they have to be, the bound alone decides.
A program may use at most 64 MiB of HBM per device.

v0:
```python
import jax
import jax.numpy as jnp
from jax import lax
from jax.sharding import PartitionSpec as P

REACH1 = 4


highest = lax.Precision.HIGHEST


def with_halo(block, sides, width):
    for axis, dim in sides:
        count = lax.axis_size(axis)
        forward = [(i, i + 1) for i in range(count - 1)]
        backward = [(target, source) for source, target in forward]
        low = lax.ppermute(
            lax.slice_in_dim(block, block.shape[dim] - width, None, axis=dim), axis, forward
        )
        high = lax.ppermute(lax.slice_in_dim(block, 0, width, axis=dim), axis, backward)
        block = jnp.concatenate([low, block, high], axis=dim)
    return block


def from_behind(value, axis, steps):
    count = lax.axis_size(axis)
    leading, last = (max(0, -steps), min(count, count - steps))
    return lax.ppermute(value, axis, [(source, source + steps) for source in range(leading, last)])


def per_device(
    rhs,
    ridge,
    leaf_basis,
    leaf_transfer,
    near_blocks,
    near_list,
    leaf_coupling,
    leaf_far,
    node_coupling,
    node_far,
):
    leaves_here = leaf_basis.shape[0]
    leaf_size = leaf_basis.shape[1]
    rank_size = leaf_basis.shape[2]
    columns = rhs.shape[0]
    device = lax.axis_index("pts")
    window_start = device * leaves_here - leaves_here
    leaf_rhs = rhs.reshape(columns, leaves_here, leaf_size)
    slots = jnp.arange(3 * leaves_here, dtype=jnp.int32)
    widened = with_halo(rhs, (("pts", 1),), rhs.shape[1])
    near_window = widened.reshape(columns, 3 * leaves_here, leaf_size)
    near_onehot = ((near_list - window_start)[..., None] == slots).astype(jnp.float32)
    near_points = jnp.einsum("ljw,cwp->ljcp", near_onehot, near_window, precision=highest)
    near_part = jnp.einsum("ljcp,ljpq->clq", near_points, near_blocks, precision=highest)
    moments = jnp.einsum("clp,lpr->lcr", leaf_rhs, leaf_basis, precision=highest)
    moment_window = with_halo(moments, (("pts", 0),), leaves_here)
    far_onehot = ((leaf_far - window_start)[..., None] == slots).astype(jnp.float32)
    far_sources = jnp.einsum("lkw,wcr->lkcr", far_onehot, moment_window, precision=highest)
    leaf_field = jnp.einsum("lkcr,lkrs->lcs", far_sources, leaf_coupling, precision=highest)
    node_moment = jnp.einsum("lcr,lrs->cs", moments, leaf_transfer, precision=highest)
    partners = node_far[0]
    relative = partners - device
    node_sources = jnp.zeros((partners.shape[0], columns, rank_size), jnp.float32)
    for offset in [value for value in range(-REACH1, REACH1 + 1) if abs(value) >= 2]:
        arrived = from_behind(node_moment, "pts", -offset)
        node_sources = node_sources + jnp.where(
            (relative == offset)[:, None, None], arrived[None], 0.0
        )
    node_field = jnp.einsum("kcr,krs->cs", node_sources, node_coupling[0], precision=highest)
    leaf_total = leaf_field + jnp.einsum(
        "cs,lrs->lcr", node_field, leaf_transfer, precision=highest
    )
    far_part = jnp.einsum("lcr,lpr->clp", leaf_total, leaf_basis, precision=highest)
    product = (far_part + near_part).reshape(columns, leaves_here * leaf_size) + ridge[
        None, :
    ] * rhs
    return product


def solution(mesh):
    in_specs = (
        P(None, "pts"),
        P("pts"),
        P("pts", None, None),
        P("pts", None, None),
        P("pts", None, None, None),
        P("pts", None),
        P("pts", None, None, None),
        P("pts", None),
        P("pts", None, None, None),
        P("pts", None),
    )
    out_specs = P(None, "pts")
    return jax.shard_map(
        per_device, mesh=mesh, in_specs=in_specs, out_specs=out_specs, check_vma=False
    )
```

profile of v0, /device:TPU:24, one launch (start us, length us, event | category | flops | bytes accessed | tf_op | source)
XLA Modules:
  0.0 72.5 jit_solution(1144047582021486726)
XLA Ops:
  0.0 0.0 copy-start
  0.0 2.2 %fusion.20 = f32[4,64,256]{2,1,0:T(8,128)S(1)} fusion(f32[4,256,256]{2,1,0:T(8,128)} %param.12, f32[8,4,8,256]{3,2,1,0:T(8,128)} %bitcast.62), kind=kOutput, calls=%fused_computation.26 | convolution fusion | flops 201326592 | bytes 1572864 | tf_op jit(solution)/shard_map/clp,lpr->lcr/dot_general | solution.py:56
  2.2 2.5 %convolution_bitcast_fusion.3 = f32[64,256]{1,0:T(8,128)} fusion(f32[4,64,256]{2,1,0:T(8,128)S(1)} %fusion.20, f32[4,256,256]{2,1,0:T(8,128)} %param.13), kind=kOutput, calls=%fused_computation.8 | convolution fusion | flops 201326592 | bytes 1376256 | tf_op jit(solution)/shard_map/lcr,lrs->cs/dot_general | solution.py:61
  4.7 10.6 %collective-permute-start.7 = (f32[64,256]{1,0:T(8,128)}, f32[64,256]{1,0:T(8,128)S(1)}, u32[]{:S(2)}, u32[]{:S(2)}) collective-permute-start(f32[64,256]{1,0:T(8,128)} %convolution_bitcast_fusion.3), channel_id=1, source_target_pairs={{4,0},{5,1},{6,2},{7,3},{8,4},{9,5},{10,6},{11,7},{12,8},{13,9},{1... | collective-permute-start | bytes 196616 | tf_op jit(solution)/shard_map/ppermute | solution.py:28
  15.3 2.5 %collective-permute-start.6 = (f32[64,256]{1,0:T(8,128)}, f32[64,256]{1,0:T(8,128)S(1)}, u32[]{:S(2)}, u32[]{:S(2)}) collective-permute-start(f32[64,256]{1,0:T(8,128)} %convolution_bitcast_fusion.3), channel_id=1, source_target_pairs={{3,0},{4,1},{5,2},{6,3},{7,4},{8,5},{9,6},{10,7},{11,8},{12,9},{13... | collective-permute-start | bytes 196616 | tf_op jit(solution)/shard_map/ppermute | solution.py:28
  17.8 2.3 %collective-permute-start.5 = (f32[64,256]{1,0:T(8,128)}, f32[64,256]{1,0:T(8,128)}, u32[]{:S(2)}, u32[]{:S(2)}) collective-permute-start(f32[64,256]{1,0:T(8,128)} %convolution_bitcast_fusion.3), channel_id=1, source_target_pairs={{2,0},{3,1},{4,2},{5,3},{6,4},{7,5},{8,6},{9,7},{10,8},{11,9},{12,... | collective-permute-start | bytes 196616 | tf_op jit(solution)/shard_map/ppermute | solution.py:28
  20.2 3.5 %collective-permute-start.4 = (f32[64,256]{1,0:T(8,128)}, f32[64,256]{1,0:T(8,128)}, u32[]{:S(2)}, u32[]{:S(2)}) collective-permute-start(f32[64,256]{1,0:T(8,128)} %convolution_bitcast_fusion.3), channel_id=1, source_target_pairs={{0,2},{1,3},{2,4},{3,5},{4,6},{5,7},{6,8},{7,9},{8,10},{9,11},{10,... | collective-permute-start | bytes 196616 | tf_op jit(solution)/shard_map/ppermute | solution.py:28
  23.7 2.5 %collective-permute-start.3 = (f32[64,256]{1,0:T(8,128)}, f32[64,256]{1,0:T(8,128)}, u32[]{:S(2)}, u32[]{:S(2)}) collective-permute-start(f32[64,256]{1,0:T(8,128)} %convolution_bitcast_fusion.3), channel_id=1, source_target_pairs={{0,3},{1,4},{2,5},{3,6},{4,7},{5,8},{6,9},{7,10},{8,11},{9,12},{10... | collective-permute-start | bytes 196616 | tf_op jit(solution)/shard_map/ppermute | solution.py:28
  26.2 0.7 broadcast_subtract_fusion
  26.9 0.7 broadcast_subtract_fusion.1
  27.6 0.7 compare_bitcast_fusion.5
  28.2 0.0 collective-permute-done.7
  28.2 2.8 %collective-permute-start.2 = (f32[64,256]{1,0:T(8,128)}, f32[64,256]{1,0:T(8,128)S(1)}, u32[]{:S(2)}, u32[]{:S(2)}) collective-permute-start(f32[64,256]{1,0:T(8,128)} %convolution_bitcast_fusion.3), channel_id=1, source_target_pairs={{0,4},{1,5},{2,6},{3,7},{4,8},{5,9},{6,10},{7,11},{8,12},{9,13},{1... | collective-permute-start | bytes 196616 | tf_op jit(solution)/shard_map/ppermute | solution.py:28
  31.1 0.0 collective-permute-done.6
  31.1 9.2 %collective-permute-start.1 = (f32[4,64,256]{2,1,0:T(8,128)S(1)}, f32[4,64,256]{2,1,0:T(8,128)S(1)}, u32[]{:S(2)}, u32[]{:S(2)}) collective-permute-start(f32[4,64,256]{2,1,0:T(8,128)S(1)} %fusion.20), channel_id=1, source_target_pairs={{1,0},{2,1},{3,2},{4,3},{5,4},{6,5},{7,6},{8,7},{9,8},{10,9},{11,1... | collective-permute-start | bytes 786440 | tf_op jit(solution)/shard_map/ppermute | solution.py:20
  40.3 0.0 collective-permute-done.5
  40.3 1.9 %collective-permute-start = (f32[4,64,256]{2,1,0:T(8,128)S(1)}, f32[4,64,256]{2,1,0:T(8,128)S(1)}, u32[]{:S(2)}, u32[]{:S(2)}) collective-permute-start(f32[4,64,256]{2,1,0:T(8,128)S(1)} %fusion.20), channel_id=1, source_target_pairs={{0,1},{1,2},{2,3},{3,4},{4,5},{5,6},{6,7},{7,8},{8,9},{9,10},{10,1... | collective-permute-start | bytes 786440 | tf_op jit(solution)/shard_map/ppermute | solution.py:17
  42.3 0.0 collective-permute-done.4
  42.3 7.9 %collective-permute-start.9 = (f32[64,1024]{1,0:T(8,128)}, f32[64,1024]{1,0:T(8,128)S(1)}, u32[]{:S(2)}, u32[]{:S(2)}) collective-permute-start(f32[64,1024]{1,0:T(8,128)} %param.10), channel_id=1, source_target_pairs={{1,0},{2,1},{3,2},{4,3},{5,4},{6,5},{7,6},{8,7},{9,8},{10,9},{11,1... | collective-permute-start | bytes 786440 | tf_op jit(solution)/shard_map/ppermute | solution.py:20
  50.1 0.0 collective-permute-done.3
  50.1 1.9 %collective-permute-start.8 = (f32[64,1024]{1,0:T(8,128)}, f32[64,1024]{1,0:T(8,128)S(1)}, u32[]{:S(2)}, u32[]{:S(2)}) collective-permute-start(f32[64,1024]{1,0:T(8,128)} %param.10), channel_id=1, source_target_pairs={{0,1},{1,2},{2,3},{3,4},{4,5},{5,6},{6,7},{7,8},{8,9},{9,10},{10,1... | collective-permute-start | bytes 786440 | tf_op jit(solution)/shard_map/ppermute | solution.py:17
  52.1 0.0 collective-permute-done.2
  52.1 0.0 copy-start.2
  52.1 2.6 %fusion = f32[64,256,1]{1,0,2:T(8,128)S(1)} fusion(f32[1,6,256,256]{3,2,1,0:T(8,128)} %param.18, f32[64,256]{1,0:T(8,128)S(1)} %collective-permute-done.7, f32[64,256]{1,0:T(8,128)S(1)} %collective-permute-done.6, f32[64,256]{1,0:T(8,128)} %collective-permute-done.5, f32[64,256]{1,0:T(8,128)} %collective-permute-done.4, f32[64,256]{1,0:T(8,128)} %collective-permute-done.3, ...), kind=kOutput, calls=%fused_computation | convolution fusion | flops 303071232 | bytes 2031652 | tf_op jit(solution)/shard_map/kcr,krs->cs/dot_general | solution.py:70
  54.7 2.3 %convolution_bitcast_fusion = f32[4,64,256]{2,1,0:T(8,128)S(1)} fusion(f32[64,256,1]{1,0,2:T(8,128)S(1)} %fusion, f32[4,256,256]{2,1,0:T(8,128)} %param.13), kind=kOutput, calls=%fused_computation.2 | convolution fusion | flops 201326592 | bytes 1376256 | tf_op jit(solution)/shard_map/cs,lrs->lcr/dot_general | solution.py:71
  57.1 0.0 collective-permute-done.1
  57.1 0.0 collective-permute-done
  57.1 0.1 maximum_bitcast_fusion
  57.1 1.3 %fusion.6 = f32[4,4,64,256]{3,1,2,0:T(4,128)S(1)} fusion(f32[12,64,256,1]{2,1,0,3:T(8,128)S(1)} %maximum_bitcast_fusion, s32[4,4]{1,0:T(4,128)S(1)} %broadcast_subtract_fusion.1), kind=kOutput, calls=%fused_computation.10 | convolution fusion | flops 37748928 | bytes 1835072 | tf_op jit(solution)/shard_map/lkw,wcr->lkcr/dot_general | solution.py:59
  58.4 0.0 copy-done.2
  58.5 0.0 copy-start.1
  58.5 0.0 copy-start.3
  58.5 2.8 %fusion.2 = f32[4,64,256]{2,1,0:T(8,128)S(1)} fusion(f32[4,64,256]{2,1,0:T(8,128)S(1)} %convolution_bitcast_fusion, f32[4,4,256,256]{3,2,1,0:T(8,128)S(1)} %copy-done.2, f32[4,4,64,256]{3,1,2,0:T(4,128)S(1)} %fusion.6), kind=kOutput, calls=%fused_computation.4 | convolution fusion | flops 805371904 | bytes 5767168 | tf_op jit(solution)/shard_map/lkcr,lkrs->lcs/dot_general | solution.py:60
  61.3 0.0 copy-done.1
  61.3 1.8 %fusion.44 = f32[4,64,256]{2,1,0:T(8,128)} fusion(f32[4,64,256]{2,1,0:T(8,128)S(1)} %fusion.2, f32[4,256,256]{2,1,0:T(8,128)S(1)} %copy-done.1), kind=kOutput, calls=%fused_computation.60 | convolution fusion | flops 201326592 | bytes 1572864 | tf_op jit(solution)/shard_map/lcr,lpr->clp/dot_general | solution.py:74
  63.1 0.0 collective-permute-done.9
  63.1 0.0 collective-permute-done.8
  63.1 0.0 copy-done.3
  63.1 1.0 %pad_maximum_fusion = f32[64,3072]{1,0:T(8,128)} fusion(f32[64,1024]{1,0:T(8,128)S(1)} %collective-permute-done.9, f32[64,1024]{1,0:T(8,128)S(1)} %copy-done.3, f32[64,1024]{1,0:T(8,128)S(1)} %collective-permute-done.8), kind=kLoop, calls=%fused_computation.13 | loop fusion | flops 393216 | bytes 1572864 | tf_op jit(solution)/shard_map/concatenate | solution.py:21
  64.1 2.3 %reshape.68 = f32[64,12,256,1]{2,1,0,3:T(8,128)} reshape(f32[64,3072]{1,0:T(8,128)} %pad_maximum_fusion) | data formatting | bytes 1572864 | tf_op jit(solution)/shard_map/reshape | solution.py:52
  66.4 0.0 copy-start.4
  66.4 2.2 %fusion.39 = f32[4,3,64,256]{3,1,2,0:T(4,128)S(1)} fusion(f32[64,12,256,1]{2,1,0,3:T(8,128)} %reshape.68, s32[4,3]{1,0:T(4,128)S(1)} %broadcast_subtract_fusion), kind=kOutput, calls=%fused_computation.47 | convolution fusion | flops 28311696 | bytes 1572912 | tf_op jit(solution)/shard_map/ljw,cwp->ljcp/dot_general | solution.py:54
  68.6 0.0 copy-done
  68.7 3.1 %fusion.4 = f32[4,8,8,256]{3,2,1,0:T(8,128)S(1)} fusion(f32[4,64,256]{2,1,0:T(8,128)} %fusion.44, f32[4,3,256,256]{3,2,1,0:T(8,128)S(1)} %copy-done, f32[4,3,64,256]{3,1,2,0:T(4,128)S(1)} %fusion.39), kind=kOutput, calls=%fused_computation.7 | convolution fusion | flops 604045312 | bytes 4456448 | tf_op jit(solution)/shard_map/ljcp,ljpq->clq/dot_general | solution.py:55
  71.7 0.0 copy-done.4
  71.8 0.7 %multiply_add_fusion = f32[64,1024]{1,0:T(8,128)} fusion(f32[64,1024]{1,0:T(8,128)S(1)} %bitcast.63, f32[64,1024]{1,0:T(8,128)S(1)} %copy-done.3, f32[1024]{0:T(1024)S(1)} %copy-done.4), kind=kLoop, calls=%fused_computation.29 | loop fusion | flops 131072 | bytes 790528 | tf_op jit(solution)/shard_map/add | solution.py:75
  (2 shorter events, 0.0 us)
Async XLA Ops:
  0.0 68.7 %copy-start = (f32[4,3,256,256]{3,2,1,0:T(8,128)S(1)}, f32[4,3,256,256]{3,2,1,0:T(8,128)}, u32[]{:S(2)}) copy-start(f32[4,3,256,256]{3,2,1,0:T(8,128)} %param.14) | copy-start | bytes 9437188
  4.7 23.5 %collective-permute-start.7 = (f32[64,256]{1,0:T(8,128)}, f32[64,256]{1,0:T(8,128)S(1)}, u32[]{:S(2)}, u32[]{:S(2)}) collective-permute-start(f32[64,256]{1,0:T(8,128)} %convolution_bitcast_fusion.3), channel_id=1, source_target_pairs={{4,0},{5,1},{6,2},{7,3},{8,4},{9,5},{10,6},{11,7},{12,8},{13,9},{1... | collective-permute-start | bytes 196616 | tf_op jit(solution)/shard_map/ppermute | solution.py:28
  15.3 15.8 %collective-permute-start.6 = (f32[64,256]{1,0:T(8,128)}, f32[64,256]{1,0:T(8,128)S(1)}, u32[]{:S(2)}, u32[]{:S(2)}) collective-permute-start(f32[64,256]{1,0:T(8,128)} %convolution_bitcast_fusion.3), channel_id=1, source_target_pairs={{3,0},{4,1},{5,2},{6,3},{7,4},{8,5},{9,6},{10,7},{11,8},{12,9},{13... | collective-permute-start | bytes 196616 | tf_op jit(solution)/shard_map/ppermute | solution.py:28
  17.8 22.5 %collective-permute-start.5 = (f32[64,256]{1,0:T(8,128)}, f32[64,256]{1,0:T(8,128)}, u32[]{:S(2)}, u32[]{:S(2)}) collective-permute-start(f32[64,256]{1,0:T(8,128)} %convolution_bitcast_fusion.3), channel_id=1, source_target_pairs={{2,0},{3,1},{4,2},{5,3},{6,4},{7,5},{8,6},{9,7},{10,8},{11,9},{12,... | collective-permute-start | bytes 196616 | tf_op jit(solution)/shard_map/ppermute | solution.py:28
  20.2 22.1 %collective-permute-start.4 = (f32[64,256]{1,0:T(8,128)}, f32[64,256]{1,0:T(8,128)}, u32[]{:S(2)}, u32[]{:S(2)}) collective-permute-start(f32[64,256]{1,0:T(8,128)} %convolution_bitcast_fusion.3), channel_id=1, source_target_pairs={{0,2},{1,3},{2,4},{3,5},{4,6},{5,7},{6,8},{7,9},{8,10},{9,11},{10,... | collective-permute-start | bytes 196616 | tf_op jit(solution)/shard_map/ppermute | solution.py:28
  23.7 26.5 %collective-permute-start.3 = (f32[64,256]{1,0:T(8,128)}, f32[64,256]{1,0:T(8,128)}, u32[]{:S(2)}, u32[]{:S(2)}) collective-permute-start(f32[64,256]{1,0:T(8,128)} %convolution_bitcast_fusion.3), channel_id=1, source_target_pairs={{0,3},{1,4},{2,5},{3,6},{4,7},{5,8},{6,9},{7,10},{8,11},{9,12},{10... | collective-permute-start | bytes 196616 | tf_op jit(solution)/shard_map/ppermute | solution.py:28
  28.2 23.9 %collective-permute-start.2 = (f32[64,256]{1,0:T(8,128)}, f32[64,256]{1,0:T(8,128)S(1)}, u32[]{:S(2)}, u32[]{:S(2)}) collective-permute-start(f32[64,256]{1,0:T(8,128)} %convolution_bitcast_fusion.3), channel_id=1, source_target_pairs={{0,4},{1,5},{2,6},{3,7},{4,8},{5,9},{6,10},{7,11},{8,12},{9,13},{1... | collective-permute-start | bytes 196616 | tf_op jit(solution)/shard_map/ppermute | solution.py:28
  31.1 26.0 %collective-permute-start.1 = (f32[4,64,256]{2,1,0:T(8,128)S(1)}, f32[4,64,256]{2,1,0:T(8,128)S(1)}, u32[]{:S(2)}, u32[]{:S(2)}) collective-permute-start(f32[4,64,256]{2,1,0:T(8,128)S(1)} %fusion.20), channel_id=1, source_target_pairs={{1,0},{2,1},{3,2},{4,3},{5,4},{6,5},{7,6},{8,7},{9,8},{10,9},{11,1... | collective-permute-start | bytes 786440 | tf_op jit(solution)/shard_map/ppermute | solution.py:20
  40.3 16.7 %collective-permute-start = (f32[4,64,256]{2,1,0:T(8,128)S(1)}, f32[4,64,256]{2,1,0:T(8,128)S(1)}, u32[]{:S(2)}, u32[]{:S(2)}) collective-permute-start(f32[4,64,256]{2,1,0:T(8,128)S(1)} %fusion.20), channel_id=1, source_target_pairs={{0,1},{1,2},{2,3},{3,4},{4,5},{5,6},{6,7},{7,8},{8,9},{9,10},{10,1... | collective-permute-start | bytes 786440 | tf_op jit(solution)/shard_map/ppermute | solution.py:17
  42.3 20.8 %collective-permute-start.9 = (f32[64,1024]{1,0:T(8,128)}, f32[64,1024]{1,0:T(8,128)S(1)}, u32[]{:S(2)}, u32[]{:S(2)}) collective-permute-start(f32[64,1024]{1,0:T(8,128)} %param.10), channel_id=1, source_target_pairs={{1,0},{2,1},{3,2},{4,3},{5,4},{6,5},{7,6},{8,7},{9,8},{10,9},{11,1... | collective-permute-start | bytes 786440 | tf_op jit(solution)/shard_map/ppermute | solution.py:20
  50.1 12.9 %collective-permute-start.8 = (f32[64,1024]{1,0:T(8,128)}, f32[64,1024]{1,0:T(8,128)S(1)}, u32[]{:S(2)}, u32[]{:S(2)}) collective-permute-start(f32[64,1024]{1,0:T(8,128)} %param.10), channel_id=1, source_target_pairs={{0,1},{1,2},{2,3},{3,4},{4,5},{5,6},{6,7},{7,8},{8,9},{9,10},{10,1... | collective-permute-start | bytes 786440 | tf_op jit(solution)/shard_map/ppermute | solution.py:17
  52.1 6.4 %copy-start.2 = (f32[4,4,256,256]{3,2,1,0:T(8,128)S(1)}, f32[4,4,256,256]{3,2,1,0:T(8,128)}, u32[]{:S(2)}) copy-start(f32[4,4,256,256]{3,2,1,0:T(8,128)} %param.16) | copy-start | bytes 12582916
  58.5 2.8 %copy-start.1 = (f32[4,256,256]{2,1,0:T(8,128)S(1)}, f32[4,256,256]{2,1,0:T(8,128)}, u32[]{:S(2)}) copy-start(f32[4,256,256]{2,1,0:T(8,128)} %param.12) | copy-start | bytes 3145732
  58.5 4.6 %copy-start.3 = (f32[64,1024]{1,0:T(8,128)S(1)}, f32[64,1024]{1,0:T(8,128)}, u32[]{:S(2)}) copy-start(f32[64,1024]{1,0:T(8,128)} %param.10) | copy-start | bytes 786436
  66.4 5.3 %copy-start.4 = (f32[1024]{0:T(1024)S(1)}, f32[1024]{0:T(1024)}, u32[]{:S(2)}) copy-start(f32[1024]{0:T(1024)} %param.11) | copy-start | bytes 12292
where the time goes:
time: 73 us; the launch traced here: 72.5 us
  starting transfers between devices  45.2 us (62%)
  matrix products  20.8 us (28%)
  other arithmetic  3.84 us (5%)
  local copies, waits for them, and re-layouts  2.39 us (3%)
    ppermute x6, starting transfers between devices, from_behind(): lax.ppermute(value, axis, [(source, source + steps) for source in range(l...  24.2 us
    ppermute x2, starting transfers between devices, with_halo(): lax.ppermute(lax.slice_in_dim(block, 0, width, axis=dim), axis, backward)  17.1 us
    ppermute x2, starting transfers between devices, with_halo(): lax.ppermute(lax.slice_in_dim(block, block.shape[dim] - width, None, axis...  3.84 us
    dot_general x1, matrix products, per_device(): jnp.einsum('ljcp,ljpq->clq', near_points, near_blocks, precision=highest)  3.06 us
    dot_general x1, matrix products, per_device(): jnp.einsum('lkcr,lkrs->lcs', far_sources, leaf_coupling, precision=highest)  2.78 us
    dot_general x1, matrix products, per_device(): jnp.einsum('kcr,krs->cs', node_sources, node_coupling[0], precision=highest)  2.6 us
    dot_general x1, matrix products, per_device(): jnp.einsum('lcr,lrs->cs', moments, leaf_transfer, precision=highest)  2.5 us
    reshape x1, local copies, waits for them, and re-layouts, per_device(): near_window = widened.reshape(columns, 3 * leaves_here, leaf_size)  2.34 us
  transfers between devices with their start and end apart: 10, of which 0 were waited for; matrix products, arithmetic and copies ran while one was open for 18% of the time, Pallas kernels for 0%

commit v1 on v0

v1 whole, which is shorter than its diff:
```python
import jax
import jax.numpy as jnp
from jax import lax
from jax.experimental import pallas as pl
from jax.experimental.pallas import tpu as pltpu
from jax.sharding import PartitionSpec as P

F32 = jnp.float32
BF16 = jnp.bfloat16
MESH = pl.DeviceIdType.MESH


def split(value):
    high = value.astype(BF16)
    low = (value - high.astype(F32)).astype(BF16)
    return high, low


def stacked(value):
    high, low = split(value)
    return jnp.concatenate([high, low], axis=0)


def product(left, weight, transposed=False):
    rows = left.shape[0] // 2
    high, low = split(weight)
    dims = (((1,), (1 if transposed else 0,)), ((), ()))
    both = lax.dot_general(left, high, dims, preferred_element_type=F32)
    rest = lax.dot_general(left[:rows], low, dims, preferred_element_type=F32)
    return both[:rows] + (both[rows:] + rest)


def inside(index, extent):
    return jnp.minimum(jnp.maximum(index, 0), extent - 1)


def kernel(
    count,
    rhs,
    basis_hbm,
    transfer_hbm,
    near_hbm,
    near_list_hbm,
    coupling_hbm,
    leaf_far_hbm,
    node_coupling_hbm,
    node_far_hbm,
    out,
    x_window,
    m_window,
    n_own,
    n_window,
    basis,
    transfer,
    near,
    coupling,
    node_coupling,
    near_list,
    leaf_far,
    node_far,
    load_sem,
    list_sem,
    send_sem,
    recv_sem,
):
    leaves = basis.shape[0]
    size = basis.shape[1]
    me = lax.axis_index("pts")
    parity = lax.rem(me, 2)
    right = lax.rem(me + 1, count)
    left = lax.rem(me + count - 1, count)
    right2 = lax.rem(me + 2, count)
    left2 = lax.rem(me + count - 2, count)
    partner = me + 1 - 2 * parity
    first = me * leaves - leaves

    def cols(l):
        return slice(l * size, (l + 1) * size)

    barrier = pltpu.get_barrier_semaphore()
    for other in (left, right, left2, right2):
        pl.semaphore_signal(barrier, inc=1, device_id=(other,), device_id_type=MESH)

    loads = {}

    def load(name, source, target, slot):
        copy = pltpu.make_async_copy(source, target, load_sem.at[slot])
        copy.start()
        loads[name] = copy

    slot = 0
    for l in range(leaves):
        load(("x", l), rhs.at[:, cols(l)], x_window.at[leaves + l], slot)
        load(("b", l), basis_hbm.at[l], basis.at[l], slot + 1)
        slot += 2
    for l in range(leaves):
        load(("t", l), transfer_hbm.at[l], transfer.at[l], slot)
        slot += 1
    lists = [
        pltpu.make_async_copy(near_list_hbm, near_list, list_sem.at[0]),
        pltpu.make_async_copy(leaf_far_hbm, leaf_far, list_sem.at[1]),
        pltpu.make_async_copy(node_far_hbm, node_far, list_sem.at[2]),
    ]
    for copy in lists:
        copy.start()
    for l in range(leaves):
        load(("n", l), near_hbm.at[l], near.at[l], slot)
        slot += 1
    load(("k", 0), node_coupling_hbm.at[0], node_coupling, slot)
    slot += 1
    for l in range(leaves):
        load(("c", l), coupling_hbm.at[l], coupling.at[l], slot)
        slot += 1

    pl.semaphore_wait(barrier, 4)

    def send(source, target, number, device):
        copy = pltpu.make_async_remote_copy(
            src_ref=source,
            dst_ref=target,
            send_sem=send_sem.at[number],
            recv_sem=recv_sem.at[number],
            device_id=(device,),
            device_id_type=MESH,
        )
        copy.start()
        return copy

    x_copies = []
    for i in range(leaves):
        a = leaves - 1 - i
        x_copies.append(send(rhs.at[:, cols(a)], x_window.at[a], 2 * i, right))
        x_copies.append(
            send(rhs.at[:, cols(i)], x_window.at[2 * leaves + i], 2 * i + 1, left)
        )

    node = None
    for l in range(leaves):
        loads["x", l].wait()
        loads["b", l].wait()
        moment = product(stacked(x_window[leaves + l]), basis[l])
        m_window[leaves + l] = moment
        loads["t", l].wait()
        term = product(stacked(moment), transfer[l])
        node = term if node is None else node + term
    n_own[...] = node

    base = 2 * leaves
    n_right = send(n_own, n_window.at[2], base, right2)
    n_left = send(n_own, n_window.at[3], base + 1, left2)
    base += 2
    m_copies = []
    for i in range(leaves):
        a = leaves - 1 - i
        m_copies.append(send(m_window.at[leaves + a], m_window.at[a], base + 2 * i, right))
        m_copies.append(
            send(m_window.at[leaves + i], m_window.at[2 * leaves + i], base + 2 * i + 1, left)
        )
    base += 2 * leaves

    for l in range(leaves):
        loads["n", l].wait()
        out[:, cols(l)] = product(stacked(x_window[leaves + l]), near[l, 0])

    n_right.wait_recv()
    n_left.wait_recv()
    relay_right = send(n_window.at[2], n_window.at[0], base, right2)
    relay_left = send(n_window.at[3], n_window.at[5], base + 1, left2)
    across = send(n_window.at[2 + parity], n_window.at[1 + 3 * parity], base + 2, partner)
    base += 3

    for copy in x_copies:
        copy.wait_recv()
    for copy in lists:
        copy.wait()
    for l in range(leaves):
        total = out[:, cols(l)]
        for j in range(1, near.shape[1]):
            source = inside(near_list[l, j] - first, 3 * leaves)
            total = total + product(stacked(x_window[source]), near[l, j])
        out[:, cols(l)] = total

    relay_right.wait_recv()
    relay_left.wait_recv()
    across2 = send(n_window.at[5 - 5 * parity], n_window.at[4 - 3 * parity], base, partner)
    loads["k", 0].wait()
    across.wait_recv()
    across2.wait_recv()
    field = None
    for k in range(node_coupling.shape[0]):
        offset = node_far[0, k] - me
        source = inside(jnp.where(offset < 0, offset + 4, offset + 1), 6)
        term = product(stacked(n_window[source]), node_coupling[k])
        field = term if field is None else field + term
    field = stacked(field)

    for copy in m_copies:
        copy.wait_recv()
    for l in range(leaves):
        loads["c", l].wait()
        total = product(field, transfer[l], transposed=True)
        for k in range(coupling.shape[1]):
            source = inside(leaf_far[l, k] - first, 3 * leaves)
            total = total + product(stacked(m_window[source]), coupling[l, k])
        out[:, cols(l)] = out[:, cols(l)] + product(stacked(total), basis[l], transposed=True)

    for copy in x_copies + m_copies + [n_right, n_left, relay_right, relay_left, across, across2]:
        copy.wait_send()


def per_device(
    rhs,
    ridge,
    leaf_basis,
    leaf_transfer,
    near_blocks,
    near_list,
    leaf_coupling,
    leaf_far,
    node_coupling,
    node_far,
):
    leaves, size, rank = leaf_basis.shape
    columns = rhs.shape[0]
    count = lax.axis_size("pts")
    in_hbm = pl.BlockSpec(memory_space=pltpu.HBM)
    vmem = pl.BlockSpec(memory_space=pltpu.VMEM)
    copies = 4 * leaves + 6
    result = pl.pallas_call(
        lambda *refs: kernel(count, *refs),
        out_shape=jax.ShapeDtypeStruct((columns, leaves * size), F32),
        in_specs=[in_hbm] * 9,
        out_specs=vmem,
        scratch_shapes=[
            pltpu.VMEM((3 * leaves, columns, size), F32),
            pltpu.VMEM((3 * leaves, columns, rank), F32),
            pltpu.VMEM((columns, rank), F32),
            pltpu.VMEM((6, columns, rank), F32),
            pltpu.VMEM(leaf_basis.shape, F32),
            pltpu.VMEM(leaf_transfer.shape, F32),
            pltpu.VMEM(near_blocks.shape, F32),
            pltpu.VMEM(leaf_coupling.shape, F32),
            pltpu.VMEM(node_coupling.shape[1:], F32),
            pltpu.SMEM(near_list.shape, jnp.int32),
            pltpu.SMEM(leaf_far.shape, jnp.int32),
            pltpu.SMEM(node_far.shape, jnp.int32),
            pltpu.SemaphoreType.DMA((5 * leaves + 1,)),
            pltpu.SemaphoreType.DMA((3,)),
            pltpu.SemaphoreType.DMA((copies,)),
            pltpu.SemaphoreType.DMA((copies,)),
        ],
        compiler_params=pltpu.CompilerParams(
            collective_id=0, has_side_effects=True, vmem_limit_bytes=66486272
        ),
    )(
        rhs,
        leaf_basis,
        leaf_transfer,
        near_blocks,
        near_list,
        leaf_coupling,
        leaf_far,
        node_coupling,
        node_far,
    )
    return result + ridge[None, :] * rhs


def solution(mesh):
    in_specs = (
        P(None, "pts"),
        P("pts"),
        P("pts", None, None),
        P("pts", None, None),
        P("pts", None, None, None),
        P("pts", None),
        P("pts", None, None, None),
        P("pts", None),
        P("pts", None, None, None),
        P("pts", None),
    )
    return jax.shard_map(
        per_device, mesh=mesh, in_specs=in_specs, out_specs=P(None, "pts"), check_vma=False
    )
```

time: 73 us -> 34.9 us (0.48)
  the two profiles are of different devices: /device:TPU:24 before, /device:TPU:1 now
where the time goes in v1:
time: 34.9 us; the launch traced here: 34.8 us
  Pallas kernels  33 us (95%)
  other arithmetic  1.69 us (5%)
    pallas_call x1, Pallas kernels, per_device(): pl.pallas_call(lambda *refs: kernel(count, *refs), out_shape=jax.ShapeDty...  33 us
    add x1, other arithmetic, per_device(): return result + ridge[None, :] * rhs  1.69 us

profile of v1, /device:TPU:1, one launch (start us, length us, event | category | flops | bytes accessed | tf_op | source)
XLA Modules:
  0.0 34.8 jit_solution(1874543763139407578)
XLA Ops:
  0.0 0.0 copy-start
  0.0 0.0 copy-start.1
  0.0 33.0 %shard_map.100 = f32[64,1024]{1,0:T(8,128)} custom-call(f32[64,1024]{1,0:T(8,128)} %refs_0_.1, f32[4,256,256]{2,1,0:T(8,128)} %refs_1_.1, f32[4,256,256]{2,1,0:T(8,128)} %refs_2_.1, f32[4,3,256,256]{3,2,1,0:T(8,128)} %refs_3_.1, s32[4,3]{1,0:T(4,128)} %refs_4_.1, f32[4,4,256,256]{3,2,1,0:T(8,128)} %refs_5_.1, s32[4,4]{1,0:T(4,128)} %refs_6_.1, ...), custom_call_target="tpu_custom_call" | custom-call | tf_op jit(solution)/shard_map/pallas_call | solution.py:229
  33.0 0.0 copy-done
  33.1 0.0 copy-done.1
  33.1 1.7 %multiply_add_fusion = f32[64,1024]{1,0:T(8,128)} fusion(f32[64,1024]{1,0:T(8,128)} %shard_map.100, f32[64,1024]{1,0:T(8,128)S(1)} %copy-done, f32[1024]{0:T(1024)S(1)} %copy-done.1), kind=kLoop, calls=%fused_computation | loop fusion | flops 131072 | bytes 790528 | tf_op jit(solution)/shard_map/add | solution.py:266
Async XLA Ops:
  0.0 33.0 %copy-start = (f32[64,1024]{1,0:T(8,128)S(1)}, f32[64,1024]{1,0:T(8,128)}, u32[]{:S(2)}) copy-start(f32[64,1024]{1,0:T(8,128)} %refs_0_.1) | copy-start | bytes 786436
  0.0 33.1 %copy-start.1 = (f32[1024]{0:T(1024)S(1)}, f32[1024]{0:T(1024)}, u32[]{:S(2)}) copy-start(f32[1024]{0:T(1024)} %param.11) | copy-start | bytes 12292

commit v2 on v1

v2 whole, which is shorter than its diff:
```python
import jax
import jax.numpy as jnp
from jax import lax
from jax.experimental import pallas as pl
from jax.experimental.pallas import tpu as pltpu
from jax.sharding import PartitionSpec as P

F32 = jnp.float32
BF16 = jnp.bfloat16
MESH = pl.DeviceIdType.MESH

COLUMN = 16


def split(value):
    high = value.astype(BF16)
    low = (value - high.astype(F32)).astype(BF16)
    return high, low


def stacked(value):
    high, low = split(value)
    return jnp.concatenate([high, low], axis=0)


def halves(left, high, low, transposed=False):
    rows = left.shape[0] // 2
    dims = (((1,), (1 if transposed else 0,)), ((), ()))
    both = lax.dot_general(left, high, dims, preferred_element_type=F32)
    rest = lax.dot_general(left[:rows], low, dims, preferred_element_type=F32)
    return both[:rows] + (both[rows:] + rest)


def product(left, weight):
    return halves(left, *split(weight))


def inside(index, extent):
    return jnp.minimum(jnp.maximum(index, 0), extent - 1)


def flag(condition):
    return condition.astype(jnp.int32).astype(F32)


def kernel(
    count,
    rhs,
    basis_hbm,
    transfer_hbm,
    near_hbm,
    near_list_hbm,
    coupling_hbm,
    leaf_far_hbm,
    node_coupling_hbm,
    node_far_hbm,
    out,
    x_window,
    x_last,
    m_window,
    m_last,
    n_own,
    n_window,
    field_sum,
    basis,
    transfer,
    near,
    coupling,
    node_coupling,
    basis_parts,
    transfer_parts,
    last_parts,
    node_parts,
    near_list,
    leaf_far,
    node_far,
    load_sem,
    send_sem,
    recv_sem,
):
    leaves, size = basis.shape[:2]
    inner = 3 * leaves - 2
    me = lax.axis_index("pts")
    parity = lax.rem(me, 2)
    chip = me // 2
    chips = count // 2
    even = parity == 0
    odd = parity == 1
    has_left = me >= 1
    has_right = me < count - 1
    near_chip_left = chip >= 1
    near_chip_right = chip < chips - 1
    far_chip_left = chip >= 2
    far_chip_right = chip < chips - 2
    right = jnp.minimum(me + 1, count - 1)
    left = jnp.maximum(me - 1, 0)
    right2 = jnp.minimum(me + 2, count - 1)
    left2 = jnp.maximum(me - 2, 0)
    right_first = lax.rem(me, COLUMN) < 4
    partner = me + 1 - 2 * parity
    first = me * leaves - leaves

    def cols(l):
        return slice(l * size, (l + 1) * size)

    barrier = pltpu.get_barrier_semaphore()
    expected = 0
    for other, there in (
        (left, has_left),
        (right, has_right),
        (left2, near_chip_left),
        (right2, near_chip_right),
    ):
        expected = expected + there.astype(jnp.int32)

        @pl.when(there)
        def _(other=other):
            pl.semaphore_signal(barrier, inc=1, device_id=(other,), device_id_type=MESH)

    def load(source, target, number):
        copy = pltpu.make_async_copy(source, target, load_sem.at[number])
        copy.start()
        return copy

    x_loads = [load(rhs.at[:, cols(l)], x_window.at[leaves - 1 + l], l) for l in range(leaves)]
    basis_loads = [load(basis_hbm.at[l], basis.at[l], leaves + l) for l in range(leaves)]
    transfer_loads = [
        load(transfer_hbm.at[l], transfer.at[l], 2 * leaves + l) for l in range(leaves)
    ]
    base = 3 * leaves
    list_loads = [
        load(near_list_hbm, near_list, base),
        load(leaf_far_hbm, leaf_far, base + 1),
        load(node_far_hbm, node_far, base + 2),
    ]
    node_load = load(node_coupling_hbm.at[0], node_coupling, base + 5)
    near_load = load(near_hbm, near, base + 3)
    coupling_load = load(coupling_hbm, coupling, base + 4)

    pl.semaphore_wait(barrier, expected)

    def remote(source, target, number, device):
        return pltpu.make_async_remote_copy(
            src_ref=source,
            dst_ref=target,
            send_sem=send_sem.at[number],
            recv_sem=recv_sem.at[number],
            device_id=(device,),
            device_id_type=MESH,
        )

    end = leaves - 1
    x_right = [
        remote(rhs.at[:, cols(l)], x_window.at[l - 1], 11 + l, right) for l in range(end, 0, -1)
    ]
    x_left = [
        remote(rhs.at[:, cols(l)], x_window.at[2 * leaves - 1 + l], 11 + leaves + l, left)
        for l in range(end)
    ]
    m_right = remote(m_window.at[leaves : 2 * leaves - 1], m_window.at[0:end], 2, right)
    m_left = remote(m_window.at[end : 2 * end], m_window.at[2 * leaves - 1 : inner], 3, left)
    m_last_right = remote(m_window.at[end], m_last.at[0], 4, right)
    m_last_left = remote(m_window.at[2 * end], m_last.at[1], 5, left)
    x_last_right = remote(rhs.at[:, cols(0)], x_last.at[0], 6, right)
    x_last_left = remote(rhs.at[:, cols(end)], x_last.at[1], 7, left)
    n_right = remote(n_own, n_window.at[2], 8, right2)
    n_left = remote(n_own, n_window.at[3], 9, left2)
    relay_right = remote(n_window.at[2], n_window.at[0], 10, right2)
    relay_left = remote(n_window.at[3], n_window.at[5], 11, left2)
    low_early = remote(n_window.at[2], n_window.at[1], 0, partner)
    low_late = remote(n_window.at[0], n_window.at[1], 0, partner)
    high_early = remote(n_window.at[3], n_window.at[4], 1, partner)
    high_late = remote(n_window.at[5], n_window.at[4], 1, partner)

    def if_start(condition, *copies):
        @pl.when(condition)
        def _():
            for copy in copies:
                copy.start()

    def if_arrived(condition, *copies):
        @pl.when(condition)
        def _():
            for copy in copies:
                copy.wait_recv()

    if_start(has_right, *x_right)
    if_start(has_left, *x_left)

    node = None
    for l in range(leaves):
        x_loads[l].wait()
        basis_loads[l].wait()
        high, low = split(basis[l])
        basis_parts[l, 0] = high
        basis_parts[l, 1] = low
        moment = halves(stacked(x_window[end + l]), high, low)
        m_window[end + l] = moment
        transfer_loads[l].wait()
        high, low = split(transfer[l])
        transfer_parts[l, 0] = high
        transfer_parts[l, 1] = low
        term = halves(stacked(moment), high, low)
        node = term if node is None else node + term
    n_own[...] = node

    if_start(near_chip_right, n_right)
    if_start(near_chip_left, n_left)
    if_start(has_right, m_right)
    if_start(has_left, m_left)

    for copy in list_loads:
        copy.wait()
    node_load.wait()
    entries = node_coupling.shape[0]
    for s, offset in enumerate((-4, -3, -2, 2, 3, 4)):
        total = None
        for k in range(entries):
            term = flag(node_far[0, k] == me + offset) * node_coupling[k]
            total = term if total is None else total + term
        node_parts[s, 0], node_parts[s, 1] = split(total)

    for l in range(leaves):
        left_parts = jnp.concatenate([basis_parts[l, 0], basis_parts[l, 1]], axis=0)
        both = halves(left_parts, transfer_parts[l, 0], transfer_parts[l, 1])
        transfer_parts[l, 0], transfer_parts[l, 1] = split(both)

    near_load.wait()
    for l in range(leaves):
        out[:, cols(l)] = product(stacked(x_window[end + l]), near[l, 0])

    def from_left():
        @pl.when(near_chip_left)
        def _():
            n_right.wait_recv()
            if_start(near_chip_right, relay_right)
            if_start(even, low_early)

        if_start(has_right, m_last_right, x_last_right)

    def from_right():
        @pl.when(near_chip_right)
        def _():
            n_left.wait_recv()
            if_start(near_chip_left, relay_left)
            if_start(odd, high_early)

        if_start(has_left, m_last_left, x_last_left)

    def in_order(one, other):
        @pl.when(right_first)
        def _():
            other()
            one()

        @pl.when(jnp.logical_not(right_first))
        def _():
            one()
            other()

    in_order(from_left, from_right)

    coupling_load.wait()
    ends = ((0, 0, first), (1, end, first + 3 * leaves - 1))
    for side, l, source in ends:
        total = flag(near_list[l, 1] == source) * near[l, 1]
        for j in range(2, near.shape[1]):
            total = total + flag(near_list[l, j] == source) * near[l, j]
        last_parts[side, 0], last_parts[side, 1] = split(total)
        total = flag(leaf_far[l, 0] == source) * coupling[l, 0]
        for k in range(1, coupling.shape[1]):
            total = total + flag(leaf_far[l, k] == source) * coupling[l, k]
        last_parts[side, 2], last_parts[side, 3] = split(total)

    def chosen(window, leaf, l):
        slot = leaf - first - 1
        value = window[inside(slot, inner)]
        if l == 0:
            value = value * flag(slot >= 0)
        if l == end:
            value = value * flag(slot < inner)
        return stacked(value)

    if_arrived(has_left, *x_right)
    if_arrived(has_right, *x_left)
    for l in range(leaves):
        total = out[:, cols(l)]
        for j in range(1, near.shape[1]):
            total = total + product(chosen(x_window, near_list[l, j], l), near[l, j])
        out[:, cols(l)] = total

    if_arrived(has_left, m_right)
    if_arrived(has_right, m_left)
    for l in range(leaves):
        total = None
        for k in range(coupling.shape[1]):
            term = product(chosen(m_window, leaf_far[l, k], l), coupling[l, k])
            total = term if total is None else total + term
        total = halves(stacked(total), basis_parts[l, 0], basis_parts[l, 1], True)
        out[:, cols(l)] = out[:, cols(l)] + total

    def node_term(s, there):
        value = stacked(jnp.where(there, n_window[s], 0.0))
        return halves(value, node_parts[s, 0], node_parts[s, 1])

    field_sum[...] = node_term(2, near_chip_left) + node_term(3, near_chip_right)

    def later_left():
        @pl.when(far_chip_left)
        def _():
            relay_right.wait_recv()
            if_start(odd, low_late)

    def later_right():
        @pl.when(far_chip_right)
        def _():
            relay_left.wait_recv()
            if_start(even, high_late)

    in_order(later_left, later_right)
    field_sum[...] = (
        field_sum[...] + node_term(0, far_chip_left) + node_term(5, far_chip_right)
    )

    if_arrived(has_left, m_last_right)
    if_arrived(has_right, m_last_left)

    def last(buffer, side):
        return stacked(jnp.where((has_left, has_right)[side], buffer[side], 0.0))

    for side, l in ((0, 0), (1, end)):
        total = halves(last(m_last, side), last_parts[side, 2], last_parts[side, 3])
        total = halves(stacked(total), basis_parts[l, 0], basis_parts[l, 1], True)
        out[:, cols(l)] = out[:, cols(l)] + total

    low_there = chip >= 2 - parity
    high_there = chip < chips - 1 - parity
    if_arrived(low_there, low_early)
    if_arrived(high_there, high_early)
    field = stacked(field_sum[...] + node_term(1, low_there) + node_term(4, high_there))
    for l in range(leaves):
        term = halves(field, transfer_parts[l, 0], transfer_parts[l, 1], True)
        out[:, cols(l)] = out[:, cols(l)] + term

    if_arrived(has_left, x_last_right)
    if_arrived(has_right, x_last_left)
    for side, l in ((0, 0), (1, end)):
        parts = last_parts[side, 0], last_parts[side, 1]
        out[:, cols(l)] = out[:, cols(l)] + halves(last(x_last, side), *parts)

    def if_sent(condition, *copies):
        @pl.when(condition)
        def _():
            for copy in copies:
                copy.wait_send()

    if_sent(has_right, *x_right, m_right, m_last_right, x_last_right)
    if_sent(has_left, *x_left, m_left, m_last_left, x_last_left)
    if_sent(near_chip_right, n_right)
    if_sent(near_chip_left, n_left)
    if_sent(near_chip_left & near_chip_right, relay_right, relay_left)
    if_sent(chip >= 1 + parity, low_early)
    if_sent(chip < chips - 2 + parity, high_early)


def per_device(
    rhs,
    ridge,
    leaf_basis,
    leaf_transfer,
    near_blocks,
    near_list,
    leaf_coupling,
    leaf_far,
    node_coupling,
    node_far,
):
    leaves, size, rank = leaf_basis.shape
    columns = rhs.shape[0]
    count = lax.axis_size("pts")
    in_hbm = pl.BlockSpec(memory_space=pltpu.HBM)
    in_vmem = pl.BlockSpec(memory_space=pltpu.VMEM)
    inner = 3 * leaves - 2
    operands = (
        rhs,
        leaf_basis,
        leaf_transfer,
        near_blocks,
        near_list,
        leaf_coupling,
        leaf_far,
        node_coupling,
        node_far,
    )
    result = pl.pallas_call(
        lambda *refs: kernel(count, *refs),
        out_shape=pltpu.VMEM((columns, leaves * size), F32),
        in_specs=[in_hbm] * len(operands),
        out_specs=in_vmem,
        scratch_shapes=[
            pltpu.VMEM((inner, columns, size), F32),
            pltpu.VMEM((2, columns, size), F32),
            pltpu.VMEM((inner, columns, rank), F32),
            pltpu.VMEM((2, columns, rank), F32),
            pltpu.VMEM((columns, rank), F32),
            pltpu.VMEM((6, columns, rank), F32),
            pltpu.VMEM((columns, rank), F32),
            pltpu.VMEM(leaf_basis.shape, F32),
            pltpu.VMEM(leaf_transfer.shape, F32),
            pltpu.VMEM(near_blocks.shape, F32),
            pltpu.VMEM(leaf_coupling.shape, F32),
            pltpu.VMEM(node_coupling.shape[1:], F32),
            pltpu.VMEM((leaves, 2, size, rank), BF16),
            pltpu.VMEM((leaves, 2, rank, rank), BF16),
            pltpu.VMEM((2, 4, size, size), BF16),
            pltpu.VMEM((6, 2, rank, rank), BF16),
            pltpu.SMEM(near_list.shape, jnp.int32),
            pltpu.SMEM(leaf_far.shape, jnp.int32),
            pltpu.SMEM(node_far.shape, jnp.int32),
            pltpu.SemaphoreType.DMA((3 * leaves + 6,)),
            pltpu.SemaphoreType.DMA((11 + 2 * leaves,)),
            pltpu.SemaphoreType.DMA((11 + 2 * leaves,)),
        ],
        compiler_params=pltpu.CompilerParams(
            collective_id=0, has_side_effects=True, vmem_limit_bytes=24 * 2**20
        ),
    )(*[pltpu.with_memory_space_constraint(value, pltpu.HBM) for value in operands])
    return result + ridge[None, :] * rhs


def solution(mesh):
    in_specs = (
        P(None, "pts"),
        P("pts"),
        P("pts", None, None),
        P("pts", None, None),
        P("pts", None, None, None),
        P("pts", None),
        P("pts", None, None, None),
        P("pts", None),
        P("pts", None, None, None),
        P("pts", None),
    )
    return jax.shard_map(
        per_device, mesh=mesh, in_specs=in_specs, out_specs=P(None, "pts"), check_vma=False
    )
```

time: 34.9 us -> 20.6 us (0.59)
  the two profiles are of different devices: /device:TPU:1 before, /device:TPU:24 now
where the time goes in v2:
time: 20.6 us; the launch traced here: 20.3 us
  Pallas kernels  19.5 us (95%)
  other arithmetic  0.74 us (4%)
    pallas_call x1, Pallas kernels, per_device(): pl.pallas_call(lambda *refs: kernel(count, *refs), out_shape=pltpu.VMEM((...  19.5 us
    add x1, other arithmetic, per_device(): return result + ridge[None, :] * rhs  0.74 us

profile of v2, /device:TPU:24, one launch (start us, length us, event | category | flops | bytes accessed | tf_op | source)
XLA Modules:
  0.0 20.3 jit_solution(5495502383871723908)
XLA Ops:
  0.0 0.0 copy-start
  0.0 0.0 copy-start.1
  0.0 19.5 %shard_map.100 = f32[64,1024]{1,0:T(8,128)S(1)} custom-call(f32[64,1024]{1,0:T(8,128)} %refs_0_.1, f32[4,256,256]{2,1,0:T(8,128)} %refs_1_.1, f32[4,256,256]{2,1,0:T(8,128)} %refs_2_.1, f32[4,3,256,256]{3,2,1,0:T(8,128)} %refs_3_.1, s32[4,3]{1,0:T(4,128)} %refs_4_.1, f32[4,4,256,256]{3,2,1,0:T(8,128)} %refs_5_.1, s32[4,4]{1,0:T(4,128)} %refs_6_.1, ...), custom_call_target="tpu_custom_call" | custom-call | tf_op jit(solution)/shard_map/pallas_call | solution.py:395
  19.5 0.0 copy-done
  19.6 0.0 copy-done.1
  19.6 0.7 %multiply_add_fusion = f32[64,1024]{1,0:T(8,128)} fusion(f32[64,1024]{1,0:T(8,128)S(1)} %shard_map.100, f32[64,1024]{1,0:T(8,128)S(1)} %copy-done, f32[1024]{0:T(1024)S(1)} %copy-done.1), kind=kLoop, calls=%fused_computation | loop fusion | flops 131072 | bytes 790528 | tf_op jit(solution)/shard_map/add | solution.py:428
Async XLA Ops:
  0.0 19.5 %copy-start = (f32[64,1024]{1,0:T(8,128)S(1)}, f32[64,1024]{1,0:T(8,128)}, u32[]{:S(2)}) copy-start(f32[64,1024]{1,0:T(8,128)} %refs_0_.1) | copy-start | bytes 786436
  0.0 19.6 %copy-start.1 = (f32[1024]{0:T(1024)S(1)}, f32[1024]{0:T(1024)}, u32[]{:S(2)}) copy-start(f32[1024]{0:T(1024)} %param.11) | copy-start | bytes 12292

commit v3 on v2

--- a/solution.py
+++ b/solution.py
@@ -9,7 +9,7 @@
 BF16 = jnp.bfloat16
 MESH = pl.DeviceIdType.MESH
 
-COLUMN = 16
+COLUMN = 8
 
 
 def split(value):
@@ -96,7 +96,9 @@
     left = jnp.maximum(me - 1, 0)
     right2 = jnp.minimum(me + 2, count - 1)
     left2 = jnp.maximum(me - 2, 0)
-    right_first = lax.rem(me, COLUMN) < 4
+    place = lax.rem(chip, COLUMN)
+    right_first = place < 2
+    relays = near_chip_left & near_chip_right
     partner = me + 1 - 2 * parity
     first = me * leaves - leaves
 
@@ -122,28 +124,26 @@
         copy.start()
         return copy
 
-    x_loads = [load(rhs.at[:, cols(l)], x_window.at[leaves - 1 + l], l) for l in range(leaves)]
-    basis_loads = [load(basis_hbm.at[l], basis.at[l], leaves + l) for l in range(leaves)]
+    for l in range(leaves):
+        load(rhs.at[:, cols(l)], x_window.at[leaves - 1 + l], 0)
+    basis_loads = [load(basis_hbm.at[l], basis.at[l], 1 + l) for l in range(leaves)]
     transfer_loads = [
-        load(transfer_hbm.at[l], transfer.at[l], 2 * leaves + l) for l in range(leaves)
+        load(transfer_hbm.at[l], transfer.at[l], 1 + leaves + l) for l in range(leaves)
     ]
-    base = 3 * leaves
+    base = 2 * leaves + 1
     list_loads = [
         load(near_list_hbm, near_list, base),
         load(leaf_far_hbm, leaf_far, base + 1),
         load(node_far_hbm, node_far, base + 2),
     ]
-    node_load = load(node_coupling_hbm.at[0], node_coupling, base + 5)
-    near_load = load(near_hbm, near, base + 3)
-    coupling_load = load(coupling_hbm, coupling, base + 4)
 
     pl.semaphore_wait(barrier, expected)
 
-    def remote(source, target, number, device):
+    def remote(source, target, number, departure, device):
         return pltpu.make_async_remote_copy(
             src_ref=source,
             dst_ref=target,
-            send_sem=send_sem.at[number],
+            send_sem=send_sem.at[departure],
             recv_sem=recv_sem.at[number],
             device_id=(device,),
             device_id_type=MESH,
@@ -151,26 +151,29 @@
 
     end = leaves - 1
     x_right = [
-        remote(rhs.at[:, cols(l)], x_window.at[l - 1], 11 + l, right) for l in range(end, 0, -1)
+        remote(x_window.at[end + l], x_window.at[l - 1], 0, 0, right) for l in range(end, 0, -1)
     ]
     x_left = [
-        remote(rhs.at[:, cols(l)], x_window.at[2 * leaves - 1 + l], 11 + leaves + l, left)
+        remote(x_window.at[end + l], x_window.at[2 * leaves - 1 + l], 1, 1, left)
         for l in range(end)
     ]
-    m_right = remote(m_window.at[leaves : 2 * leaves - 1], m_window.at[0:end], 2, right)
-    m_left = remote(m_window.at[end : 2 * end], m_window.at[2 * leaves - 1 : inner], 3, left)
-    m_last_right = remote(m_window.at[end], m_last.at[0], 4, right)
-    m_last_left = remote(m_window.at[2 * end], m_last.at[1], 5, left)
-    x_last_right = remote(rhs.at[:, cols(0)], x_last.at[0], 6, right)
-    x_last_left = remote(rhs.at[:, cols(end)], x_last.at[1], 7, left)
-    n_right = remote(n_own, n_window.at[2], 8, right2)
-    n_left = remote(n_own, n_window.at[3], 9, left2)
-    relay_right = remote(n_window.at[2], n_window.at[0], 10, right2)
-    relay_left = remote(n_window.at[3], n_window.at[5], 11, left2)
-    low_early = remote(n_window.at[2], n_window.at[1], 0, partner)
-    low_late = remote(n_window.at[0], n_window.at[1], 0, partner)
-    high_early = remote(n_window.at[3], n_window.at[4], 1, partner)
-    high_late = remote(n_window.at[5], n_window.at[4], 1, partner)
+    low, high = x_window.at[0:end], x_window.at[2 * leaves - 1 : inner]
+    x_from_left = remote(low, low, 0, 0, right)
+    x_from_right = remote(high, high, 1, 1, left)
+    m_right = remote(m_window.at[leaves : 2 * leaves - 1], m_window.at[0:end], 2, 0, right)
+    m_left = remote(m_window.at[end : 2 * end], m_window.at[2 * leaves - 1 : inner], 3, 1, left)
+    m_last_right = remote(m_window.at[end], m_last.at[0], 4, 0, right)
+    m_last_left = remote(m_window.at[2 * end], m_last.at[1], 5, 1, left)
+    x_last_right = remote(x_window.at[end], x_last.at[0], 6, 0, right)
+    x_last_left = remote(x_window.at[2 * end], x_last.at[1], 7, 1, left)
+    n_right = remote(n_own, n_window.at[2], 8, 2, right2)
+    n_left = remote(n_own, n_window.at[3], 9, 3, left2)
+    relay_right = remote(n_window.at[2], n_window.at[0], 10, 4, right2)
+    relay_left = remote(n_window.at[3], n_window.at[5], 11, 5, left2)
+    low_early = remote(n_window.at[2], n_window.at[1], 12, 6, partner)
+    low_late = remote(n_window.at[0], n_window.at[1], 12, 6, partner)
+    high_early = remote(n_window.at[3], n_window.at[4], 13, 7, partner)
+    high_late = remote(n_window.at[5], n_window.at[4], 13, 7, partner)
 
     def if_start(condition, *copies):
         @pl.when(condition)
@@ -184,12 +187,16 @@
             for copy in copies:
                 copy.wait_recv()
 
+    x_own = x_window.at[end : end + leaves]
+    pltpu.make_async_copy(x_own, x_own, load_sem.at[0]).wait()
     if_start(has_right, *x_right)
     if_start(has_left, *x_left)
+    node_load = load(node_coupling_hbm.at[0], node_coupling, base + 5)
+    near_load = load(near_hbm, near, base + 3)
+    coupling_load = load(coupling_hbm, coupling, base + 4)
 
     node = None
     for l in range(leaves):
-        x_loads[l].wait()
         basis_loads[l].wait()
         high, low = split(basis[l])
         basis_parts[l, 0] = high
@@ -281,8 +288,8 @@
             value = value * flag(slot < inner)
         return stacked(value)
 
-    if_arrived(has_left, *x_right)
-    if_arrived(has_right, *x_left)
+    if_arrived(has_left, x_from_left)
+    if_arrived(has_right, x_from_right)
     for l in range(leaves):
         total = out[:, cols(l)]
         for j in range(1, near.shape[1]):
@@ -342,25 +349,26 @@
         term = halves(field, transfer_parts[l, 0], transfer_parts[l, 1], True)
         out[:, cols(l)] = out[:, cols(l)] + term
 
+    def if_sent(condition, copy):
+        @pl.when(condition)
+        def _():
+            copy.wait_send()
+
+    everything = m_window.at[0 : 2 * leaves]
+    if_sent(has_right, remote(everything, everything, 0, 0, right))
+    if_sent(has_left, remote(everything, everything, 0, 1, left))
+    if_sent(near_chip_right, n_right)
+    if_sent(near_chip_left, n_left)
+    if_sent(relays, relay_right)
+    if_sent(relays, relay_left)
+    if_sent(chip >= 1 + parity, low_early)
+    if_sent(chip < chips - 2 + parity, high_early)
+
     if_arrived(has_left, x_last_right)
     if_arrived(has_right, x_last_left)
     for side, l in ((0, 0), (1, end)):
         parts = last_parts[side, 0], last_parts[side, 1]
         out[:, cols(l)] = out[:, cols(l)] + halves(last(x_last, side), *parts)
-
-    def if_sent(condition, *copies):
-        @pl.when(condition)
-        def _():
-            for copy in copies:
-                copy.wait_send()
-
-    if_sent(has_right, *x_right, m_right, m_last_right, x_last_right)
-    if_sent(has_left, *x_left, m_left, m_last_left, x_last_left)
-    if_sent(near_chip_right, n_right)
-    if_sent(near_chip_left, n_left)
-    if_sent(near_chip_left & near_chip_right, relay_right, relay_left)
-    if_sent(chip >= 1 + parity, low_early)
-    if_sent(chip < chips - 2 + parity, high_early)
 
 
 def per_device(
@@ -417,9 +425,9 @@
             pltpu.SMEM(near_list.shape, jnp.int32),
             pltpu.SMEM(leaf_far.shape, jnp.int32),
             pltpu.SMEM(node_far.shape, jnp.int32),
-            pltpu.SemaphoreType.DMA((3 * leaves + 6,)),
-            pltpu.SemaphoreType.DMA((11 + 2 * leaves,)),
-            pltpu.SemaphoreType.DMA((11 + 2 * leaves,)),
+            pltpu.SemaphoreType.DMA((2 * leaves + 7,)),
+            pltpu.SemaphoreType.DMA((8,)),
+            pltpu.SemaphoreType.DMA((14,)),
         ],
         compiler_params=pltpu.CompilerParams(
             collective_id=0, has_side_effects=True, vmem_limit_bytes=24 * 2**20

time: 20.6 us -> 20.5 us (level)
  no operation moved by 1% of the time
where the time goes in v3:
time: 20.5 us; the launch traced here: 20.1 us
  Pallas kernels  19.3 us (94%)
  other arithmetic  0.74 us (4%)
    pallas_call x1, Pallas kernels, per_device(): pl.pallas_call(lambda *refs: kernel(count, *refs), out_shape=pltpu.VMEM((...  19.3 us
    add x1, other arithmetic, per_device(): return result + ridge[None, :] * rhs  0.74 us

profile of v3, /device:TPU:24, one launch (start us, length us, event | category | flops | bytes accessed | tf_op | source)
XLA Modules:
  0.0 20.1 jit_solution(16948414875862290856)
XLA Ops:
  0.0 0.0 copy-start
  0.0 0.0 copy-start.1
  0.0 19.3 %shard_map.100 = f32[64,1024]{1,0:T(8,128)S(1)} custom-call(f32[64,1024]{1,0:T(8,128)} %refs_0_.1, f32[4,256,256]{2,1,0:T(8,128)} %refs_1_.1, f32[4,256,256]{2,1,0:T(8,128)} %refs_2_.1, f32[4,3,256,256]{3,2,1,0:T(8,128)} %refs_3_.1, s32[4,3]{1,0:T(4,128)} %refs_4_.1, f32[4,4,256,256]{3,2,1,0:T(8,128)} %refs_5_.1, s32[4,4]{1,0:T(4,128)} %refs_6_.1, ...), custom_call_target="tpu_custom_call" | custom-call | tf_op jit(solution)/shard_map/pallas_call | solution.py:403
  19.4 0.0 copy-done
  19.4 0.0 copy-done.1
  19.4 0.7 %multiply_add_fusion = f32[64,1024]{1,0:T(8,128)} fusion(f32[64,1024]{1,0:T(8,128)S(1)} %shard_map.100, f32[64,1024]{1,0:T(8,128)S(1)} %copy-done, f32[1024]{0:T(1024)S(1)} %copy-done.1), kind=kLoop, calls=%fused_computation | loop fusion | flops 131072 | bytes 790528 | tf_op jit(solution)/shard_map/add | solution.py:436
Async XLA Ops:
  0.0 19.4 %copy-start = (f32[64,1024]{1,0:T(8,128)S(1)}, f32[64,1024]{1,0:T(8,128)}, u32[]{:S(2)}) copy-start(f32[64,1024]{1,0:T(8,128)} %refs_0_.1) | copy-start | bytes 786436
  0.0 19.4 %copy-start.1 = (f32[1024]{0:T(1024)S(1)}, f32[1024]{0:T(1024)}, u32[]{:S(2)}) copy-start(f32[1024]{0:T(1024)} %param.11) | copy-start | bytes 12292

commit v4 on v3

--- a/solution.py
+++ b/solution.py
@@ -71,6 +71,7 @@
     transfer_parts,
     last_parts,
     node_parts,
+    coupling_parts,
     near_list,
     leaf_far,
     node_far,
@@ -189,8 +190,8 @@
 
     x_own = x_window.at[end : end + leaves]
     pltpu.make_async_copy(x_own, x_own, load_sem.at[0]).wait()
-    if_start(has_right, *x_right)
-    if_start(has_left, *x_left)
+    if_start(has_right, *x_right[:2])
+    if_start(has_left, *x_left[:2])
     node_load = load(node_coupling_hbm.at[0], node_coupling, base + 5)
     near_load = load(near_hbm, near, base + 3)
     coupling_load = load(coupling_hbm, coupling, base + 4)
@@ -213,8 +214,8 @@
 
     if_start(near_chip_right, n_right)
     if_start(near_chip_left, n_left)
-    if_start(has_right, m_right)
-    if_start(has_left, m_left)
+    if_start(has_right, x_right[2], m_right)
+    if_start(has_left, x_left[2], m_left)
 
     for copy in list_loads:
         copy.wait()
@@ -288,6 +289,10 @@
             value = value * flag(slot < inner)
         return stacked(value)
 
+    for l in range(leaves):
+        for k in range(coupling.shape[1]):
+            coupling_parts[l, k, 0], coupling_parts[l, k, 1] = split(coupling[l, k])
+
     if_arrived(has_left, x_from_left)
     if_arrived(has_right, x_from_right)
     for l in range(leaves):
@@ -301,7 +306,8 @@
     for l in range(leaves):
         total = None
         for k in range(coupling.shape[1]):
-            term = product(chosen(m_window, leaf_far[l, k], l), coupling[l, k])
+            parts = coupling_parts[l, k, 0], coupling_parts[l, k, 1]
+            term = halves(chosen(m_window, leaf_far[l, k], l), *parts)
             total = term if total is None else total + term
         total = halves(stacked(total), basis_parts[l, 0], basis_parts[l, 1], True)
         out[:, cols(l)] = out[:, cols(l)] + total
@@ -422,6 +428,7 @@
             pltpu.VMEM((leaves, 2, rank, rank), BF16),
             pltpu.VMEM((2, 4, size, size), BF16),
             pltpu.VMEM((6, 2, rank, rank), BF16),
+            pltpu.VMEM(leaf_coupling.shape[:2] + (2, rank, rank), BF16),
             pltpu.SMEM(near_list.shape, jnp.int32),
             pltpu.SMEM(leaf_far.shape, jnp.int32),
             pltpu.SMEM(node_far.shape, jnp.int32),
@@ -430,7 +437,7 @@
             pltpu.SemaphoreType.DMA((14,)),
         ],
         compiler_params=pltpu.CompilerParams(
-            collective_id=0, has_side_effects=True, vmem_limit_bytes=24 * 2**20
+            collective_id=0, has_side_effects=True, vmem_limit_bytes=30 * 2**20
         ),
     )(*[pltpu.with_memory_space_constraint(value, pltpu.HBM) for value in operands])
     return result + ridge[None, :] * rhs

time: 20.5 us -> 20.4 us (level)
  no operation moved by 1% of the time
where the time goes in v4:
time: 20.4 us; the launch traced here: 20.1 us
  Pallas kernels  19.3 us (95%)
  other arithmetic  0.74 us (4%)
    pallas_call x1, Pallas kernels, per_device(): pl.pallas_call(lambda *refs: kernel(count, *refs), out_shape=pltpu.VMEM((...  19.3 us
    add x1, other arithmetic, per_device(): return result + ridge[None, :] * rhs  0.74 us

profile of v4, /device:TPU:24, one launch (start us, length us, event | category | flops | bytes accessed | tf_op | source)
XLA Modules:
  0.0 20.1 jit_solution(4244483974682427477)
XLA Ops:
  0.0 0.0 copy-start
  0.0 0.0 copy-start.1
  0.0 19.3 %shard_map.100 = f32[64,1024]{1,0:T(8,128)S(1)} custom-call(f32[64,1024]{1,0:T(8,128)} %refs_0_.1, f32[4,256,256]{2,1,0:T(8,128)} %refs_1_.1, f32[4,256,256]{2,1,0:T(8,128)} %refs_2_.1, f32[4,3,256,256]{3,2,1,0:T(8,128)} %refs_3_.1, s32[4,3]{1,0:T(4,128)} %refs_4_.1, f32[4,4,256,256]{3,2,1,0:T(8,128)} %refs_5_.1, s32[4,4]{1,0:T(4,128)} %refs_6_.1, ...), custom_call_target="tpu_custom_call" | custom-call | tf_op jit(solution)/shard_map/pallas_call | solution.py:409
  19.4 0.0 copy-done
  19.4 0.0 copy-done.1
  19.4 0.7 %multiply_add_fusion = f32[64,1024]{1,0:T(8,128)} fusion(f32[64,1024]{1,0:T(8,128)S(1)} %shard_map.100, f32[64,1024]{1,0:T(8,128)S(1)} %copy-done, f32[1024]{0:T(1024)S(1)} %copy-done.1), kind=kLoop, calls=%fused_computation | loop fusion | flops 131072 | bytes 790528 | tf_op jit(solution)/shard_map/add | solution.py:443
Async XLA Ops:
  0.0 19.4 %copy-start = (f32[64,1024]{1,0:T(8,128)S(1)}, f32[64,1024]{1,0:T(8,128)}, u32[]{:S(2)}) copy-start(f32[64,1024]{1,0:T(8,128)} %refs_0_.1) | copy-start | bytes 786436
  0.0 19.4 %copy-start.1 = (f32[1024]{0:T(1024)S(1)}, f32[1024]{0:T(1024)}, u32[]{:S(2)}) copy-start(f32[1024]{0:T(1024)} %param.11) | copy-start | bytes 12292

commit v5 on v4

--- a/solution.py
+++ b/solution.py
@@ -128,10 +128,8 @@
     for l in range(leaves):
         load(rhs.at[:, cols(l)], x_window.at[leaves - 1 + l], 0)
     basis_loads = [load(basis_hbm.at[l], basis.at[l], 1 + l) for l in range(leaves)]
-    transfer_loads = [
-        load(transfer_hbm.at[l], transfer.at[l], 1 + leaves + l) for l in range(leaves)
-    ]
-    base = 2 * leaves + 1
+    transfer_load = load(transfer_hbm, transfer, 1 + leaves)
+    base = leaves + 2
     list_loads = [
         load(near_list_hbm, near_list, base),
         load(leaf_far_hbm, leaf_far, base + 1),
@@ -204,7 +202,8 @@
         basis_parts[l, 1] = low
         moment = halves(stacked(x_window[end + l]), high, low)
         m_window[end + l] = moment
-        transfer_loads[l].wait()
+        if l == 0:
+            transfer_load.wait()
         high, low = split(transfer[l])
         transfer_parts[l, 0] = high
         transfer_parts[l, 1] = low
@@ -432,7 +431,7 @@
             pltpu.SMEM(near_list.shape, jnp.int32),
             pltpu.SMEM(leaf_far.shape, jnp.int32),
             pltpu.SMEM(node_far.shape, jnp.int32),
-            pltpu.SemaphoreType.DMA((2 * leaves + 7,)),
+            pltpu.SemaphoreType.DMA((leaves + 8,)),
             pltpu.SemaphoreType.DMA((8,)),
             pltpu.SemaphoreType.DMA((14,)),
         ],

time: 20.4 us -> 20.5 us (level)
  no operation moved by 1% of the time
where the time goes in v5:
time: 20.5 us; the launch traced here: 20.2 us
  Pallas kernels  19.5 us (95%)
  other arithmetic  0.74 us (4%)
    pallas_call x1, Pallas kernels, per_device(): pl.pallas_call(lambda *refs: kernel(count, *refs), out_shape=pltpu.VMEM((...  19.5 us
    add x1, other arithmetic, per_device(): return result + ridge[None, :] * rhs  0.74 us

profile of v5, /device:TPU:24, one launch (start us, length us, event | category | flops | bytes accessed | tf_op | source)
XLA Modules:
  0.0 20.2 jit_solution(17616621467037500545)
XLA Ops:
  0.0 0.0 copy-start
  0.0 0.0 copy-start.1
  0.0 19.5 %shard_map.100 = f32[64,1024]{1,0:T(8,128)S(1)} custom-call(f32[64,1024]{1,0:T(8,128)} %refs_0_.1, f32[4,256,256]{2,1,0:T(8,128)} %refs_1_.1, f32[4,256,256]{2,1,0:T(8,128)} %refs_2_.1, f32[4,3,256,256]{3,2,1,0:T(8,128)} %refs_3_.1, s32[4,3]{1,0:T(4,128)} %refs_4_.1, f32[4,4,256,256]{3,2,1,0:T(8,128)} %refs_5_.1, s32[4,4]{1,0:T(4,128)} %refs_6_.1, ...), custom_call_target="tpu_custom_call" | custom-call | tf_op jit(solution)/shard_map/pallas_call | solution.py:408
  19.5 0.0 copy-done
  19.5 0.0 copy-done.1
  19.5 0.7 %multiply_add_fusion = f32[64,1024]{1,0:T(8,128)} fusion(f32[64,1024]{1,0:T(8,128)S(1)} %shard_map.100, f32[64,1024]{1,0:T(8,128)S(1)} %copy-done, f32[1024]{0:T(1024)S(1)} %copy-done.1), kind=kLoop, calls=%fused_computation | loop fusion | flops 131072 | bytes 790528 | tf_op jit(solution)/shard_map/add | solution.py:442
Async XLA Ops:
  0.0 19.5 %copy-start = (f32[64,1024]{1,0:T(8,128)S(1)}, f32[64,1024]{1,0:T(8,128)}, u32[]{:S(2)}) copy-start(f32[64,1024]{1,0:T(8,128)} %refs_0_.1) | copy-start | bytes 786436
  0.0 19.5 %copy-start.1 = (f32[1024]{0:T(1024)S(1)}, f32[1024]{0:T(1024)}, u32[]{:S(2)}) copy-start(f32[1024]{0:T(1024)} %param.11) | copy-start | bytes 12292
